TPU v7x, 32 devices: a whole 2x2x4 slice. The times are simulated.
32 devices in a mesh: parts: 2 (over x), xline: 16 (over z, y, core).
Axes of the slice: x: 2, y: 2, z: 4, core: 2. Of those that a mesh axis runs over, the one named last changes fastest.
Arguments:
- gathers: bfloat16 [4, 96, 96, 256], P('parts', 'xline'), parts along dimension 0, may hold values from -6 to 6
- time_steps: float32 [2], replicated, may hold values from 0.3 to 0.8
- radon_op: bfloat16 [32, 2, 96, 96], P('xline'), may hold values from -0.4375 to 0.4375
Outputs:
- conditioned: bfloat16 [4, 96, 96, 256], P('parts', 'xline'), parts along dimension 0
There are 2 independent parts, one for each index of `parts`. A program takes and returns all parts, laid end to end along the dimension named above; an argument that names none is the same for every part. Nothing has to cross between parts.
All inputs are finite; a program needn't handle non-finite values.
Results may differ from a plain program's by a relative error of at most 0.0072.
Values may be sent and summed in bfloat16 or wider, within the bound.
No kernel may reach another device: no remote copies, remote signals or barrier semaphores. Data moves between devices by JAX's collectives and lax.ppermute only.
A program may use at most 128 MiB of HBM per device.

v0:
```python
import math
import jax
import jax.numpy as jnp
from jax import lax
from jax.sharding import PartitionSpec as P


def diff_depth(field):
    padded = jnp.pad(field, ((0, 0), (0, 0), (0, 0), (1, 1)))
    return 0.5 * (padded[..., 2:] - padded[..., :-2])


def box_depth(field):
    padded = jnp.pad(field, ((0, 0), (0, 0), (0, 0), (1, 1)))
    return (padded[..., :-2] + padded[..., 1:-1] + padded[..., 2:]) / 3.0


def diff_cross(field):
    return 0.5 * (field[:, 2:] - field[:, :-2])


def box_cross(field):
    return (field[:, :-2] + field[:, 1:-1] + field[:, 2:]) / 3.0


def diffuse(extended, tau_value, columns, total):
    inside = ((columns >= 0) & (columns < total)).astype(jnp.float32)[None, :, None, None]
    grad_cross = diff_cross(extended) * inside[:, 1:-1]
    grad_depth = diff_depth(extended[:, 1:-1]) * inside[:, 1:-1]
    tensor_xx = box_cross(box_depth(grad_cross * grad_cross)) * inside[:, 2:-2]
    tensor_xz = box_cross(box_depth(grad_cross * grad_depth)) * inside[:, 2:-2]
    tensor_zz = box_cross(box_depth(grad_depth * grad_depth)) * inside[:, 2:-2]
    norm_term = 1.0 + tensor_xx + tensor_zz
    inner_x = grad_cross[:, 1:-1]
    inner_z = grad_depth[:, 1:-1]
    flux_cross = inner_x - (tensor_xx * inner_x + tensor_xz * inner_z) / norm_term
    flux_depth = inner_z - (tensor_xz * inner_x + tensor_zz * inner_z) / norm_term
    change = diff_cross(flux_cross) + diff_depth(flux_depth[:, 1:-1])
    return (extended[:, 3:-3] + tau_value * change) * inside[:, 3:-3]


def forward_table(depth, bins):
    zeds = jnp.arange(depth, dtype=jnp.int32)[:, None]
    freqs = jnp.arange(bins, dtype=jnp.int32)[None, :]
    phase = (zeds * freqs % depth).astype(jnp.float32) * (2.0 * math.pi / depth)
    return jnp.concatenate([jnp.cos(phase), -jnp.sin(phase)], axis=1).astype(jnp.bfloat16)


def inverse_table(depth, bins):
    freqs = jnp.arange(bins, dtype=jnp.int32)[:, None]
    zeds = jnp.arange(depth, dtype=jnp.int32)[None, :]
    phase = (zeds * freqs % depth).astype(jnp.float32) * (2.0 * math.pi / depth)
    weight = jnp.where(freqs == 0, 1.0, 2.0).astype(jnp.float32) / depth
    return jnp.concatenate([weight * jnp.cos(phase), -weight * jnp.sin(phase)], axis=0).astype(
        jnp.bfloat16
    )


def complex_mats(operators):
    real_row = jnp.stack([operators[:, 0], -operators[:, 1]], axis=1)
    imag_row = jnp.stack([operators[:, 1], operators[:, 0]], axis=1)
    return jnp.stack([real_row, imag_row], axis=1)


def per_device(gathers, time_steps, radon_op):
    inlines, lines, offsets, depth = gathers.shape
    devices = lax.axis_size("xline")
    total = lines * devices
    bins = radon_op.shape[0] * devices
    steps_count = time_steps.shape[0]
    traces = jnp.transpose(gathers, (0, 2, 1, 3)).reshape(inlines * offsets, lines, depth)
    local_rows = lax.all_to_all(traces, "xline", split_axis=0, concat_axis=1, tiled=True)
    pair_rows = local_rows.shape[0]
    field = local_rows.astype(jnp.float32).reshape(pair_rows, total, 1, depth)
    columns = jnp.arange(-3, total + 3, dtype=jnp.int32)
    for number in range(steps_count):
        extended = jnp.pad(field, ((0, 0), (3, 3), (0, 0), (0, 0)))
        field = diffuse(extended, time_steps[number], columns, total)
    smooth = field.astype(jnp.bfloat16)
    spectrum = jnp.dot(
        smooth.reshape(-1, depth), forward_table(depth, bins), preferred_element_type=jnp.float32
    )
    spectrum = spectrum.astype(jnp.bfloat16).reshape(pair_rows, total, 2, bins)
    by_bins = lax.all_to_all(spectrum, "xline", split_axis=3, concat_axis=0, tiled=True)
    by_bins = by_bins.reshape(inlines, offsets, total, 2, radon_op.shape[0])
    mats = complex_mats(radon_op)
    done = jnp.einsum("ioxrf,fqrpo->ipxqf", by_bins, mats, preferred_element_type=jnp.float32)
    done = done.astype(jnp.bfloat16)
    back = lax.all_to_all(done, "xline", split_axis=2, concat_axis=4, tiled=True)
    filtered = jnp.transpose(back, (0, 2, 1, 3, 4))
    result = jnp.dot(
        filtered.reshape(-1, 2 * bins),
        inverse_table(depth, bins),
        preferred_element_type=jnp.float32,
    )
    return result.astype(jnp.bfloat16).reshape(inlines, lines, offsets, depth)


def solution(mesh):
    return jax.shard_map(
        per_device,
        mesh=mesh,
        in_specs=(P("parts", "xline", None, None), P(), P("xline", None, None, None)),
        out_specs=P("parts", "xline", None, None),
        check_vma=False,
    )
```

profile of v0, /device:TPU:0, one launch (start us, length us, event | category | flops | bytes accessed | tf_op | source)
XLA Modules:
  0.0 80.3 jit_solution(15486866586063491887)
XLA Ops:
  0.0 1.1 %copy.34 = bf16[2,6,96,256]{3,2,0,1:T(8,128)(2,1)S(1)} copy(bf16[2,6,96,256]{3,2,1,0:T(8,128)(2,1)} %param.3) | data formatting | bytes 1179648 | tf_op args[0]
  1.1 1.2 %copy.35 = bf16[192,6,256]{2,1,0:T(8,128)(2,1)} copy(bf16[192,6,256]{2,0,1:T(8,128)(2,1)S(1)} %bitcast.56) | data formatting | bytes 1179648 | tf_op jit(solution)/shard_map/reshape | solution.py:71
  2.3 7.4 %all-to-all-start = ((bf16[192,6,256]{2,1,0:T(8,128)(2,1)}), bf16[192,6,256]{2,1,0:T(8,128)(2,1)S(1)}, u32[]{:S(2)}, u32[]{:S(2)}) async-start(bf16[192,6,256]{2,1,0:T(8,128)(2,1)} %copy.35), calls=%async_computation | async-start | bytes 1572864 | tf_op jit(solution)/shard_map/all_to_all | solution.py:72
  9.8 0.6 fusion.81
  12.0 16.4 %all-to-all-done = bf16[192,6,256]{2,1,0:T(8,128)(2,1)S(1)} async-done(((bf16[192,6,256]{2,1,0:T(8,128)(2,1)}), bf16[192,6,256]{2,1,0:T(8,128)(2,1)S(1)}, u32[]{:S(2)}, u32[]{:S(2)}) %all-to-all-start) | async-done | bytes 589856 | tf_op jit(solution)/shard_map/all_to_all | solution.py:72
  28.7 0.7 copy.37
  29.7 0.8 fusion.79
  30.8 0.7 fusion.10
  31.6 1.4 %fusion.2 = (f32[12,100,1,256]{3,1,0,2:T(8,128)S(1)}, f32[12,100,1,256]{3,1,0,2:T(8,128)S(1)}) fusion(f32[12,100,1,256]{3,1,0,2:T(8,128)S(1)} %mul.293, f32[12,100,1,256]{3,1,0,2:T(8,128)S(1)} %get-tuple-element.16), kind=kLoop, calls=%fused_computation.24 | loop fusion | flops 1843200 | bytes 4915200 | tf_op jit(solution)/shard_map/div | solution.py:15
  33.0 2.9 %divide_subtract_fusion.1 = (f32[12,98,1,256]{3,1,0,2:T(8,128)S(1)}, f32[12,98,1,256]{3,1,0,2:T(8,128)}, f32[12,98,1,256]{3,1,0,2:T(8,128)S(1)}, f32[12,98,1,256...) fusion(f32[12,100,1,256]{3,1,0,2:T(8,128)S(1)} %get-tuple-element.18, ...), kind=kLoop, calls=%fused_computation.65 | loop fusion | flops 4816896 | bytes 20472200 | tf_op jit(solution)/shard_map/sub | solution.py:36
  36.0 1.1 %copy-done.2 = f32[12,98,1,256]{3,1,0,2:T(8,128)S(1)} copy-done((f32[12,98,1,256]{3,1,0,2:T(8,128)S(1)}, f32[12,98,1,256]{3,1,0,2:T(8,128)}, u32[]{:S(2)}) %copy-start.2) | copy-done | bytes 1204248
  37.1 0.4 copy-done.3
  37.5 0.4 copy-done.4
  37.9 0.7 fusion.41
  38.6 0.7 fusion.32
  39.5 0.8 fusion.74
  40.4 0.7 fusion.13
  41.3 0.7 fusion.21
  42.1 0.7 fusion.18
  42.8 3.0 %divide_subtract_fusion = (f32[12,98,1,256]{3,1,0,2:T(8,128)S(1)}, f32[12,98,1,256]{3,1,0,2:T(8,128)S(1)}, f32[12,98,1,256]{3,1,0,2:T(8,128)S(1)}, f32[12,98,1,2...) fusion(f32[12,100,1,256]{3,1,0,2:T(8,128)S(1)} %get-tuple-element.11, ...), kind=kLoop, calls=%fused_computation.62 | loop fusion | flops 4816896 | bytes 20472200 | tf_op jit(solution)/shard_map/sub | solution.py:36
  46.0 1.1 %copy-done = f32[12,98,1,256]{3,1,0,2:T(8,128)S(1)} copy-done((f32[12,98,1,256]{3,1,0,2:T(8,128)S(1)}, f32[12,98,1,256]{3,1,0,2:T(8,128)}, u32[]{:S(2)}) %copy-start) | copy-done | bytes 1204248
  47.1 0.4 copy-done.1
  47.5 0.7 fusion.39
  48.3 0.7 fusion.38
  49.3 0.3 reshape.81
  49.6 0.9 %copy.38 = bf16[12,96,2,32]{1,2,0,3:T(2,128)(2,1)} copy(bf16[12,96,2,32]{1,0,3,2:T(8,128)(2,1)S(1)} %reshape.81) | data formatting | bytes 294912 | tf_op jit(solution)/shard_map/reshape | solution.py:83
  50.5 5.4 %all-to-all-start.1 = ((bf16[12,96,2,32]{1,2,0,3:T(2,128)(2,1)}), bf16[12,96,2,32]{1,2,0,3:T(2,128)(2,1)S(1)}, u32[]{:S(2)}, u32[]{:S(2)}) async-start(bf16[12,96,2,32]{1,2,0,3:T(2,128)(2,1)} %copy.38), calls=%async_computation.1 | async-start | bytes 393216 | tf_op jit(solution)/shard_map/all_to_all | solution.py:84
  56.0 8.9 %all-to-all-done.1 = bf16[12,96,2,32]{1,2,0,3:T(2,128)(2,1)S(1)} async-done(((bf16[12,96,2,32]{1,2,0,3:T(2,128)(2,1)}), bf16[12,96,2,32]{1,2,0,3:T(2,128)(2,1)S(1)}, u32[]{:S(2)}, u32[]{:S(2)}) %all-to-all-start.1) | async-done | bytes 147488 | tf_op jit(solution)/shard_map/all_to_all | solution.py:84
  65.3 0.8 %copy.41 = bf16[2,96,96,2,2]{1,0,3,4,2:T(2,128)(2,1)} copy(bf16[2,96,96,2,2]{2,1,0,3,4:T(8,128)(2,1)S(1)} %fusion.44) | data formatting | bytes 294912 | tf_op jit(solution)/shard_map/convert_element_type | solution.py:88
  66.2 3.5 %all-to-all-start.2 = ((bf16[2,96,96,2,2]{1,0,3,4,2:T(2,128)(2,1)}), bf16[2,96,96,2,2]{1,0,3,4,2:T(2,128)(2,1)S(1)}, u32[]{:S(2)}, u32[]{:S(2)}) async-start(bf16[2,96,96,2,2]{1,0,3,4,2:T(2,128)(2,1)} %copy.41), calls=%async_computation.2 | async-start | bytes 393216 | tf_op jit(solution)/shard_map/all_to_all | solution.py:89
  69.9 8.8 %all-to-all-done.2 = bf16[2,96,96,2,2]{1,0,3,4,2:T(2,128)(2,1)S(1)} async-done(((bf16[2,96,96,2,2]{1,0,3,4,2:T(2,128)(2,1)}), bf16[2,96,96,2,2]{1,0,3,4,2:T(2,128)(2,1)S(1)}, u32[]{:S(2)}, u32[]{:S(2)}) %all-to-all-start.2) | async-done | bytes 147488 | tf_op jit(solution)/shard_map/all_to_all | solution.py:89
  79.2 1.2 %convolution_convert_fusion = bf16[1152,256]{1,0:T(8,128)(2,1)} fusion(bf16[1152,64]{0,1:T(8,128)(2,1)S(1)} %reshape.83, bf16[32,256]{1,0:T(8,128)(2,1)S(1)} %get-tuple-element.34, bf16[32,256]{1,0:T(8,128)(2,1)S(1)} %get-tuple-element.35), kind=kOutput, calls=%fused_computation | convolution fusion | flops 38109184 | bytes 770048 | tf_op jit(solution)/shard_map/dot_general | solution.py:91
  (36 shorter events, 3.5 us)
Async XLA Ops:
  1.1 8.7 %copy-start.6 = (f32[2]{0:T(128)S(1)}, f32[2]{0:T(128)}, u32[]{:S(2)}) copy-start(f32[2]{0:T(128)} %param.4) | copy-start | bytes 28
  2.3 26.1 %all-to-all-start = ((bf16[192,6,256]{2,1,0:T(8,128)(2,1)}), bf16[192,6,256]{2,1,0:T(8,128)(2,1)S(1)}, u32[]{:S(2)}, u32[]{:S(2)}) async-start(bf16[192,6,256]{2,1,0:T(8,128)(2,1)} %copy.35), calls=%async_computation | async-start | bytes 1572864 | tf_op jit(solution)/shard_map/all_to_all | solution.py:72
  35.8 1.3 %copy-start.2 = (f32[12,98,1,256]{3,1,0,2:T(8,128)S(1)}, f32[12,98,1,256]{3,1,0,2:T(8,128)}, u32[]{:S(2)}) copy-start(f32[12,98,1,256]{3,1,0,2:T(8,128)} %get-tuple-element.13) | copy-start | bytes 3612676
  35.8 1.7 %copy-start.3 = (f32[12,98,1,256]{3,1,0,2:T(8,128)S(1)}, f32[12,98,1,256]{3,1,0,2:T(8,128)}, u32[]{:S(2)}) copy-start(f32[12,98,1,256]{3,1,0,2:T(8,128)} %get-tuple-element.21) | copy-start | bytes 3612676
  35.8 2.1 %copy-start.4 = (f32[12,98,1,256]{3,1,0,2:T(8,128)S(1)}, f32[12,98,1,256]{3,1,0,2:T(8,128)}, u32[]{:S(2)}) copy-start(f32[12,98,1,256]{3,1,0,2:T(8,128)} %get-tuple-element.22) | copy-start | bytes 3612676
  45.8 1.3 %copy-start = (f32[12,98,1,256]{3,1,0,2:T(8,128)S(1)}, f32[12,98,1,256]{3,1,0,2:T(8,128)}, u32[]{:S(2)}) copy-start(f32[12,98,1,256]{3,1,0,2:T(8,128)} %get-tuple-element.19) | copy-start | bytes 3612676
  45.8 1.7 %copy-start.1 = (f32[12,98,1,256]{3,1,0,2:T(8,128)S(1)}, f32[12,98,1,256]{3,1,0,2:T(8,128)}, u32[]{:S(2)}) copy-start(f32[12,98,1,256]{3,1,0,2:T(8,128)} %get-tuple-element.20) | copy-start | bytes 3612676
  49.0 6.9 %copy-start.5 = (bf16[2,2,96,96]{3,2,1,0:T(8,128)(2,1)S(1)}, bf16[2,2,96,96]{3,2,1,0:T(8,128)(2,1)}, u32[]{:S(2)}) copy-start(bf16[2,2,96,96]{3,2,1,0:T(8,128)(2,1)} %param.5) | copy-start | bytes 221188
  50.5 14.3 %all-to-all-start.1 = ((bf16[12,96,2,32]{1,2,0,3:T(2,128)(2,1)}), bf16[12,96,2,32]{1,2,0,3:T(2,128)(2,1)S(1)}, u32[]{:S(2)}, u32[]{:S(2)}) async-start(bf16[12,96,2,32]{1,2,0,3:T(2,128)(2,1)} %copy.38), calls=%async_computation.1 | async-start | bytes 393216 | tf_op jit(solution)/shard_map/all_to_all | solution.py:84
  66.2 12.5 %all-to-all-start.2 = ((bf16[2,96,96,2,2]{1,0,3,4,2:T(2,128)(2,1)}), bf16[2,96,96,2,2]{1,0,3,4,2:T(2,128)(2,1)S(1)}, u32[]{:S(2)}, u32[]{:S(2)}) async-start(bf16[2,96,96,2,2]{1,0,3,4,2:T(2,128)(2,1)} %copy.41), calls=%async_computation.2 | async-start | bytes 393216 | tf_op jit(solution)/shard_map/all_to_all | solution.py:89
where the time goes:
time: 80.8 us; the launch traced here: 80.3 us
  waiting for transfers between devices  34 us (42%)
  starting transfers between devices  16.3 us (20%)
  other arithmetic  16.3 us (20%)
  local copies, waits for them, and re-layouts  10.4 us (13%)
  matrix products  1.73 us (2%)
  between operations  1.56 us (2%)
    all_to_all x1, waiting for transfers between devices, per_device(): lax.all_to_all(traces, 'xline', split_axis=0, concat_axis=1, tiled=True)  16.4 us
    all_to_all x1, waiting for transfers between devices, per_device(): lax.all_to_all(spectrum, 'xline', split_axis=3, concat_axis=0, tiled=True)  8.87 us
    all_to_all x1, waiting for transfers between devices, per_device(): lax.all_to_all(done, 'xline', split_axis=2, concat_axis=4, tiled=True)  8.76 us
    all_to_all x1, starting transfers between devices, per_device(): lax.all_to_all(traces, 'xline', split_axis=0, concat_axis=1, tiled=True)  7.41 us
    sub x2, other arithmetic, diffuse(): inner_x - (tensor_xx * inner_x + tensor_xz * inner_z) / norm_term  5.89 us
    all_to_all x1, starting transfers between devices, per_device(): lax.all_to_all(spectrum, 'xline', split_axis=3, concat_axis=0, tiled=True)  5.38 us
    unnamed x15, local copies, waits for them, and re-layouts  4.54 us
    div x5, other arithmetic, box_depth(): return (padded[..., :-2] + padded[..., 1:-1] + padded[..., 2:]) / 3.0  4.28 us
  transfers between devices with their start and end apart: 3, of which 3 were waited for; matrix products, arithmetic and copies ran while one was open for 1% of the time, Pallas kernels for 0%

commit v1 on v0

--- a/solution.py
+++ b/solution.py
@@ -3,6 +3,37 @@
 import jax.numpy as jnp
 from jax import lax
 from jax.sharding import PartitionSpec as P
+from jax.lax import axis_index, axis_size, ppermute
+
+
+def _extend_screen(local_values, where_dim, s0):
+    val = local_values.shape
+    out_arr = local_values.reshape(
+        *val[:where_dim], s0, val[where_dim] // s0, *val[where_dim + 1 :]
+    )
+    return jnp.moveaxis(out_arr, where_dim, 0)
+
+
+def choose_core(tile_in, d0):
+    odd = list(tile_in.shape[1:])
+    odd[d0] *= tile_in.shape[0]
+    return jnp.moveaxis(tile_in, 0, d0).reshape(odd)
+
+
+def open_the_pages(x_local, peer_axis, xs, z_in):
+    x_next = axis_size(peer_axis)
+    wide_out = axis_index(peer_axis)
+    plain, before = (x_next, wide_out)
+    everything = _extend_screen(x_local, xs, plain)
+    copies = [everything[before]]
+    k = 1
+    while k < plain:
+        reply = everything[before ^ k]
+        frame_out = ppermute(reply, peer_axis, [(it, it ^ k) for it in range(plain)])
+        copies.append(frame_out)
+        k = k + 1
+    everything = jnp.stack(copies, axis=0)[before ^ jnp.arange(plain)]
+    return choose_core(everything, z_in)
 
 
 def diff_depth(field):
@@ -86,7 +117,7 @@
     mats = complex_mats(radon_op)
     done = jnp.einsum("ioxrf,fqrpo->ipxqf", by_bins, mats, preferred_element_type=jnp.float32)
     done = done.astype(jnp.bfloat16)
-    back = lax.all_to_all(done, "xline", split_axis=2, concat_axis=4, tiled=True)
+    back = open_the_pages(done, "xline", 2, 4)
     filtered = jnp.transpose(back, (0, 2, 1, 3, 4))
     result = jnp.dot(
         filtered.reshape(-1, 2 * bins),

time: 80.8 us -> 92.9 us (1.15)
  starting transfers between devices: 16.3 us -> 33.9 us
  waiting for transfers between devices: 34 us -> 27.5 us
    ppermute x0 -> x15, starting transfers between devices: none -> 21.1 us  [open_the_pages(): ppermute(reply, peer_axis, [(it, it ^ k) for it in range(plain)])]
    all_to_all x1 -> x0, waiting for transfers between devices: 8.76 us -> none  [per_device(): lax.all_to_all(done, 'xline', split_axis=2, concat_axis=4, tiled=True)]
    all_to_all x1 -> x0, starting transfers between devices: 3.52 us -> none  [per_device(): lax.all_to_all(done, 'xline', split_axis=2, concat_axis=4, tiled=True)]
    ppermute x0 -> x15, waiting for transfers between devices: none -> 2.59 us  [open_the_pages(): ppermute(reply, peer_axis, [(it, it ^ k) for it in range(plain)])]
    gather x0 -> x1, local copies, waits for them, and re-layouts: none -> 0.94 us  [open_the_pages(): everything = jnp.stack(copies, axis=0)[before ^ jnp.arange(plain)]]
    unnamed x15 -> x30, local copies, waits for them, and re-layouts: 4.54 us -> 4.79 us
  transfers between devices with their start and end apart: 3 -> 17, of which waited for: 3 -> 4; matrix products, arithmetic and copies ran while one was open for 1% -> 2% of each run, Pallas kernels for 0% -> 0%
where the time goes in v1:
time: 92.9 us; the launch traced here: 92.5 us
  starting transfers between devices  33.9 us (36%)
  waiting for transfers between devices  27.5 us (30%)
  other arithmetic  16.4 us (18%)
  local copies, waits for them, and re-layouts  11.1 us (12%)
  between operations  1.8 us (2%)
  matrix products  1.73 us (2%)
    ppermute x15, starting transfers between devices, open_the_pages(): ppermute(reply, peer_axis, [(it, it ^ k) for it in range(plain)])  21.1 us
    all_to_all x1, waiting for transfers between devices, per_device(): lax.all_to_all(traces, 'xline', split_axis=0, concat_axis=1, tiled=True)  16.2 us
    all_to_all x1, waiting for transfers between devices, per_device(): lax.all_to_all(spectrum, 'xline', split_axis=3, concat_axis=0, tiled=True)  8.72 us
    all_to_all x1, starting transfers between devices, per_device(): lax.all_to_all(traces, 'xline', split_axis=0, concat_axis=1, tiled=True)  7.41 us
    sub x2, other arithmetic, diffuse(): inner_x - (tensor_xx * inner_x + tensor_xz * inner_z) / norm_term  5.9 us
    all_to_all x1, starting transfers between devices, per_device(): lax.all_to_all(spectrum, 'xline', split_axis=3, concat_axis=0, tiled=True)  5.38 us
    unnamed x30, local copies, waits for them, and re-layouts  4.79 us
    div x5, other arithmetic, box_depth(): return (padded[..., :-2] + padded[..., 1:-1] + padded[..., 2:]) / 3.0  4.28 us
  transfers between devices with their start and end apart: 17, of which 4 were waited for; matrix products, arithmetic and copies ran while one was open for 2% of the time, Pallas kernels for 0%

profile of v1, /device:TPU:0, one launch (start us, length us, event | category | flops | bytes accessed | tf_op | source)
XLA Modules:
  0.0 92.5 jit_solution(6184504206814267926)
XLA Ops:
  0.0 1.1 %copy.31 = bf16[2,6,96,256]{3,2,0,1:T(8,128)(2,1)S(1)} copy(bf16[2,6,96,256]{3,2,1,0:T(8,128)(2,1)} %param.3) | data formatting | bytes 1179648 | tf_op args[0]
  1.1 1.2 %copy.32 = bf16[192,6,256]{2,1,0:T(8,128)(2,1)} copy(bf16[192,6,256]{2,0,1:T(8,128)(2,1)S(1)} %bitcast.120) | data formatting | bytes 1179648 | tf_op jit(solution)/shard_map/reshape | solution.py:102
  2.4 7.4 %all-to-all-start = ((bf16[192,6,256]{2,1,0:T(8,128)(2,1)}), bf16[192,6,256]{2,1,0:T(8,128)(2,1)S(1)}, u32[]{:S(2)}, u32[]{:S(2)}) async-start(bf16[192,6,256]{2,1,0:T(8,128)(2,1)} %copy.32), calls=%async_computation | async-start | bytes 1572864 | tf_op jit(solution)/shard_map/all_to_all | solution.py:103
  12.3 16.2 %all-to-all-done = bf16[192,6,256]{2,1,0:T(8,128)(2,1)S(1)} async-done(((bf16[192,6,256]{2,1,0:T(8,128)(2,1)}), bf16[192,6,256]{2,1,0:T(8,128)(2,1)S(1)}, u32[]{:S(2)}, u32[]{:S(2)}) %all-to-all-start) | async-done | bytes 589856 | tf_op jit(solution)/shard_map/all_to_all | solution.py:103
  29.7 0.8 fusion.80
  31.6 1.4 %fusion.2 = (f32[12,100,1,256]{3,1,0,2:T(8,128)S(1)}, f32[12,100,1,256]{3,1,0,2:T(8,128)S(1)}) fusion(f32[12,100,1,256]{3,1,0,2:T(8,128)S(1)} %mul.293, f32[12,100,1,256]{3,1,0,2:T(8,128)S(1)} %get-tuple-element.16), kind=kLoop, calls=%fused_computation.25 | loop fusion | flops 1843200 | bytes 4915200 | tf_op jit(solution)/shard_map/div | solution.py:46
  33.0 2.9 %divide_subtract_fusion.1 = (f32[12,98,1,256]{3,1,0,2:T(8,128)S(1)}, f32[12,98,1,256]{3,1,0,2:T(8,128)}, f32[12,98,1,256]{3,1,0,2:T(8,128)S(1)}, f32[12,98,1,256...) fusion(f32[12,100,1,256]{3,1,0,2:T(8,128)S(1)} %get-tuple-element.18, ...), kind=kLoop, calls=%fused_computation.66 | loop fusion | flops 4816896 | bytes 20472200 | tf_op jit(solution)/shard_map/sub | solution.py:67
  36.0 1.1 %copy-done.2 = f32[12,98,1,256]{3,1,0,2:T(8,128)S(1)} copy-done((f32[12,98,1,256]{3,1,0,2:T(8,128)S(1)}, f32[12,98,1,256]{3,1,0,2:T(8,128)}, u32[]{:S(2)}) %copy-start.2) | copy-done | bytes 1204248
  37.9 0.7 fusion.41
  38.7 0.7 fusion.32
  39.5 0.8 fusion.75
  40.5 0.7 fusion.13
  42.8 3.0 %divide_subtract_fusion = (f32[12,98,1,256]{3,1,0,2:T(8,128)S(1)}, f32[12,98,1,256]{3,1,0,2:T(8,128)S(1)}, f32[12,98,1,256]{3,1,0,2:T(8,128)S(1)}, f32[12,98,1,2...) fusion(f32[12,100,1,256]{3,1,0,2:T(8,128)S(1)} %get-tuple-element.11, ...), kind=kLoop, calls=%fused_computation.63 | loop fusion | flops 4816896 | bytes 20472200 | tf_op jit(solution)/shard_map/sub | solution.py:67
  46.0 1.1 %copy-done = f32[12,98,1,256]{3,1,0,2:T(8,128)S(1)} copy-done((f32[12,98,1,256]{3,1,0,2:T(8,128)S(1)}, f32[12,98,1,256]{3,1,0,2:T(8,128)}, u32[]{:S(2)}) %copy-start) | copy-done | bytes 1204248
  47.5 0.7 fusion.39
  49.6 0.9 copy.35
  50.5 5.4 %all-to-all-start.1 = ((bf16[12,96,2,32]{1,2,0,3:T(2,128)(2,1)}), bf16[12,96,2,32]{1,2,0,3:T(2,128)(2,1)S(1)}, u32[]{:S(2)}, u32[]{:S(2)}) async-start(bf16[12,96,2,32]{1,2,0,3:T(2,128)(2,1)} %copy.35), calls=%async_computation.1 | async-start | bytes 393216 | tf_op jit(solution)/shard_map/all_to_all | solution.py:115
  56.1 8.7 %all-to-all-done.1 = bf16[12,96,2,32]{1,2,0,3:T(2,128)(2,1)S(1)} async-done(((bf16[12,96,2,32]{1,2,0,3:T(2,128)(2,1)}), bf16[12,96,2,32]{1,2,0,3:T(2,128)(2,1)S(1)}, u32[]{:S(2)}, u32[]{:S(2)}) %all-to-all-start.1) | async-done | bytes 147488 | tf_op jit(solution)/shard_map/all_to_all | solution.py:115
  66.1 1.6 %collective-permute-start.2 = (bf16[2,96,6,2,2]{1,4,3,2,0:T(2,128)(2,1)S(1)}, bf16[2,96,6,2,2]{1,4,3,2,0:T(2,128)(2,1)S(1)}, u32[]{:S(2)}, u32[]{:S(2)}) collective-permute-start(bf16[2,96,6,2,2]{1,4,3,2,0:T(2,128)(2,1)S(1)} %get-tuple-element.35), channel_id=1, source_target_pairs={{0,3},{1,2},{2,1},{3,0},{4,7},{5,6},{6,5},{7,4},{8,11},{9,10},{10,... | collective-permute-start | bytes 27656 | tf_op jit(solution)/shard_map/ppermute | solution.py:32
  67.7 1.7 %collective-permute-start.4 = (bf16[2,96,6,2,2]{1,4,3,2,0:T(2,128)(2,1)S(1)}, bf16[2,96,6,2,2]{1,4,3,2,0:T(2,128)(2,1)S(1)}, u32[]{:S(2)}, u32[]{:S(2)}) collective-permute-start(bf16[2,96,6,2,2]{1,4,3,2,0:T(2,128)(2,1)S(1)} %get-tuple-element.33), channel_id=1, source_target_pairs={{0,5},{1,4},{2,7},{3,6},{4,1},{5,0},{6,3},{7,2},{8,13},{9,12},{10,... | collective-permute-start | bytes 27656 | tf_op jit(solution)/shard_map/ppermute | solution.py:32
  69.9 2.3 %collective-permute-start.6 = (bf16[2,96,6,2,2]{1,4,3,2,0:T(2,128)(2,1)S(1)}, bf16[2,96,6,2,2]{1,4,3,2,0:T(2,128)(2,1)S(1)}, u32[]{:S(2)}, u32[]{:S(2)}) collective-permute-start(bf16[2,96,6,2,2]{1,4,3,2,0:T(2,128)(2,1)S(1)} %get-tuple-element.31), channel_id=1, source_target_pairs={{0,7},{1,6},{2,5},{3,4},{4,3},{5,2},{6,1},{7,0},{8,15},{9,14},{10,... | collective-permute-start | bytes 27656 | tf_op jit(solution)/shard_map/ppermute | solution.py:32
  72.2 0.8 collective-permute-start.7
  73.0 1.9 %collective-permute-start.8 = (bf16[2,96,6,2,2]{1,4,3,2,0:T(2,128)(2,1)S(1)}, bf16[2,96,6,2,2]{1,4,3,2,0:T(2,128)(2,1)S(1)}, u32[]{:S(2)}, u32[]{:S(2)}) collective-permute-start(bf16[2,96,6,2,2]{1,4,3,2,0:T(2,128)(2,1)S(1)} %get-tuple-element.29), channel_id=1, source_target_pairs={{0,9},{1,8},{2,11},{3,10},{4,13},{5,12},{6,15},{7,14},{8,1},{9,0},... | collective-permute-start | bytes 27656 | tf_op jit(solution)/shard_map/ppermute | solution.py:32
  75.4 3.3 %collective-permute-start.10 = (bf16[2,96,6,2,2]{1,4,3,2,0:T(2,128)(2,1)S(1)}, bf16[2,96,6,2,2]{1,4,3,2,0:T(2,128)(2,1)S(1)}, u32[]{:S(2)}, u32[]{:S(2)}) collective-permute-start(bf16[2,96,6,2,2]{1,4,3,2,0:T(2,128)(2,1)S(1)} %get-tuple-element.27), channel_id=1, source_target_pairs={{0,11},{1,10},{2,9},{3,8},{4,15},{5,14},{6,13},{7,12},{8,3},{9,2},... | collective-permute-start | bytes 27656 | tf_op jit(solution)/shard_map/ppermute | solution.py:32
  78.8 0.9 collective-permute-start.11
  79.7 2.7 %collective-permute-start.12 = (bf16[2,96,6,2,2]{1,4,3,2,0:T(2,128)(2,1)S(1)}, bf16[2,96,6,2,2]{1,4,3,2,0:T(2,128)(2,1)S(1)}, u32[]{:S(2)}, u32[]{:S(2)}) collective-permute-start(bf16[2,96,6,2,2]{1,4,3,2,0:T(2,128)(2,1)S(1)} %get-tuple-element.25), channel_id=1, source_target_pairs={{0,13},{1,12},{2,15},{3,14},{4,9},{5,8},{6,11},{7,10},{8,5},{9,4},... | collective-permute-start | bytes 27656 | tf_op jit(solution)/shard_map/ppermute | solution.py:32
  82.4 1.5 %collective-permute-start.13 = (bf16[2,96,6,2,2]{1,4,3,2,0:T(2,128)(2,1)S(1)}, bf16[2,96,6,2,2]{1,4,3,2,0:T(2,128)(2,1)S(1)}, u32[]{:S(2)}, u32[]{:S(2)}) collective-permute-start(bf16[2,96,6,2,2]{1,4,3,2,0:T(2,128)(2,1)S(1)} %get-tuple-element.24), channel_id=1, source_target_pairs={{0,14},{1,15},{2,12},{3,13},{4,10},{5,11},{6,8},{7,9},{8,6},{9,7},... | collective-permute-start | bytes 27656 | tf_op jit(solution)/shard_map/ppermute | solution.py:32
  83.9 3.2 %collective-permute-start.14 = (bf16[2,96,6,2,2]{1,4,3,2,0:T(2,128)(2,1)S(1)}, bf16[2,96,6,2,2]{1,4,3,2,0:T(2,128)(2,1)S(1)}, u32[]{:S(2)}, u32[]{:S(2)}) collective-permute-start(bf16[2,96,6,2,2]{1,4,3,2,0:T(2,128)(2,1)S(1)} %get-tuple-element.23), channel_id=1, source_target_pairs={{0,15},{1,14},{2,13},{3,12},{4,11},{5,10},{6,9},{7,8},{8,7},{9,6},... | collective-permute-start | bytes 27656 | tf_op jit(solution)/shard_map/ppermute | solution.py:32
  87.2 1.7 %collective-permute-done.13 = bf16[2,96,6,2,2]{1,4,3,2,0:T(2,128)(2,1)S(1)} collective-permute-done((bf16[2,96,6,2,2]{1,4,3,2,0:T(2,128)(2,1)S(1)}, bf16[2,96,6,2,2]{1,4,3,2,0:T(2,128)(2,1)S(1)}, u32[]{:S(2)}, u32[]{:S(2)}) %collective-permute-start.13) | collective-permute-done | bytes 9248 | tf_op jit(solution)/shard_map/ppermute | solution.py:32
  88.9 0.9 collective-permute-done.14
  89.8 0.9 %gather_fusion = bf16[16,2,96,6,2,2]{2,5,4,3,1,0:T(2,128)(2,1)S(1)} fusion(bf16[16,2,96,6,2,2]{2,5,4,3,1,0:T(2,128)(2,1)S(1)} %constant_dynamic-update-slice_fusion, s32[1024]{0:T(1024)S(1)} %pad_clamp_fusion), kind=kCustom, calls=%fused_computation | custom fusion | bytes 294976 | tf_op jit(solution)/shard_map/gather | solution.py:35
  91.3 1.2 %convolution_convert_fusion = bf16[1152,256]{1,0:T(8,128)(2,1)} fusion(bf16[1152,64]{0,1:T(8,128)(2,1)S(1)} %reshape.138, bf16[32,256]{1,0:T(8,128)(2,1)S(1)} %multiply_convert_fusion, bf16[32,256]{1,0:T(8,128)(2,1)S(1)} %multiply_convert_fusion.1), kind=kOutput, calls=%fused_computation.1 | convolution fusion | flops 38109184 | bytes 770048 | tf_op jit(solution)/shard_map/dot_general | solution.py:122
  (84 shorter events, 11.3 us)
Async XLA Ops:
  1.1 8.9 %copy-start.6 = (f32[2]{0:T(128)S(1)}, f32[2]{0:T(128)}, u32[]{:S(2)}) copy-start(f32[2]{0:T(128)} %param.4) | copy-start | bytes 28
  1.1 10.7 %copy-start.5 = (bf16[2,2,96,96]{3,2,1,0:T(8,128)(2,1)S(1)}, bf16[2,2,96,96]{3,2,1,0:T(8,128)(2,1)}, u32[]{:S(2)}) copy-start(bf16[2,2,96,96]{3,2,1,0:T(8,128)(2,1)} %param.5) | copy-start | bytes 221188
  2.4 26.1 %all-to-all-start = ((bf16[192,6,256]{2,1,0:T(8,128)(2,1)}), bf16[192,6,256]{2,1,0:T(8,128)(2,1)S(1)}, u32[]{:S(2)}, u32[]{:S(2)}) async-start(bf16[192,6,256]{2,1,0:T(8,128)(2,1)} %copy.32), calls=%async_computation | async-start | bytes 1572864 | tf_op jit(solution)/shard_map/all_to_all | solution.py:103
  35.8 1.3 %copy-start.2 = (f32[12,98,1,256]{3,1,0,2:T(8,128)S(1)}, f32[12,98,1,256]{3,1,0,2:T(8,128)}, u32[]{:S(2)}) copy-start(f32[12,98,1,256]{3,1,0,2:T(8,128)} %get-tuple-element.13) | copy-start | bytes 3612676
  35.8 1.7 %copy-start.3 = (f32[12,98,1,256]{3,1,0,2:T(8,128)S(1)}, f32[12,98,1,256]{3,1,0,2:T(8,128)}, u32[]{:S(2)}) copy-start(f32[12,98,1,256]{3,1,0,2:T(8,128)} %get-tuple-element.21) | copy-start | bytes 3612676
  35.8 2.1 %copy-start.4 = (f32[12,98,1,256]{3,1,0,2:T(8,128)S(1)}, f32[12,98,1,256]{3,1,0,2:T(8,128)}, u32[]{:S(2)}) copy-start(f32[12,98,1,256]{3,1,0,2:T(8,128)} %get-tuple-element.22) | copy-start | bytes 3612676
  45.9 1.3 %copy-start = (f32[12,98,1,256]{3,1,0,2:T(8,128)S(1)}, f32[12,98,1,256]{3,1,0,2:T(8,128)}, u32[]{:S(2)}) copy-start(f32[12,98,1,256]{3,1,0,2:T(8,128)} %get-tuple-element.19) | copy-start | bytes 3612676
  45.9 1.7 %copy-start.1 = (f32[12,98,1,256]{3,1,0,2:T(8,128)S(1)}, f32[12,98,1,256]{3,1,0,2:T(8,128)}, u32[]{:S(2)}) copy-start(f32[12,98,1,256]{3,1,0,2:T(8,128)} %get-tuple-element.20) | copy-start | bytes 3612676
  50.5 14.3 %all-to-all-start.1 = ((bf16[12,96,2,32]{1,2,0,3:T(2,128)(2,1)}), bf16[12,96,2,32]{1,2,0,3:T(2,128)(2,1)S(1)}, u32[]{:S(2)}, u32[]{:S(2)}) async-start(bf16[12,96,2,32]{1,2,0,3:T(2,128)(2,1)} %copy.35), calls=%async_computation.1 | async-start | bytes 393216 | tf_op jit(solution)/shard_map/all_to_all | solution.py:115
  65.7 3.7 %collective-permute-start = (bf16[2,96,6,2,2]{1,4,3,2,0:T(2,128)(2,1)S(1)}, bf16[2,96,6,2,2]{1,4,3,2,0:T(2,128)(2,1)S(1)}, u32[]{:S(2)}, u32[]{:S(2)}) collective-permute-start(bf16[2,96,6,2,2]{1,4,3,2,0:T(2,128)(2,1)S(1)} %get-tuple-element.37), channel_id=1, source_target_pairs={{0,1},{1,0},{2,3},{3,2},{4,5},{5,4},{6,7},{7,6},{8,9},{9,8},{10,11... | collective-permute-start | bytes 27656 | tf_op jit(solution)/shard_map/ppermute | solution.py:32
  65.8 4.1 %collective-permute-start.1 = (bf16[2,96,6,2,2]{1,4,3,2,0:T(2,128)(2,1)S(1)}, bf16[2,96,6,2,2]{1,4,3,2,0:T(2,128)(2,1)S(1)}, u32[]{:S(2)}, u32[]{:S(2)}) collective-permute-start(bf16[2,96,6,2,2]{1,4,3,2,0:T(2,128)(2,1)S(1)} %get-tuple-element.36), channel_id=1, source_target_pairs={{0,2},{1,3},{2,0},{3,1},{4,6},{5,7},{6,4},{7,5},{8,10},{9,11},{10,... | collective-permute-start | bytes 27656 | tf_op jit(solution)/shard_map/ppermute | solution.py:32
  66.1 6.1 %collective-permute-start.2 = (bf16[2,96,6,2,2]{1,4,3,2,0:T(2,128)(2,1)S(1)}, bf16[2,96,6,2,2]{1,4,3,2,0:T(2,128)(2,1)S(1)}, u32[]{:S(2)}, u32[]{:S(2)}) collective-permute-start(bf16[2,96,6,2,2]{1,4,3,2,0:T(2,128)(2,1)S(1)} %get-tuple-element.35), channel_id=1, source_target_pairs={{0,3},{1,2},{2,1},{3,0},{4,7},{5,6},{6,5},{7,4},{8,11},{9,10},{10,... | collective-permute-start | bytes 27656 | tf_op jit(solution)/shard_map/ppermute | solution.py:32
  67.7 5.3 %collective-permute-start.3 = (bf16[2,96,6,2,2]{1,4,3,2,0:T(2,128)(2,1)S(1)}, bf16[2,96,6,2,2]{1,4,3,2,0:T(2,128)(2,1)S(1)}, u32[]{:S(2)}, u32[]{:S(2)}) collective-permute-start(bf16[2,96,6,2,2]{1,4,3,2,0:T(2,128)(2,1)S(1)} %get-tuple-element.34), channel_id=1, source_target_pairs={{0,4},{1,5},{2,6},{3,7},{4,0},{5,1},{6,2},{7,3},{8,12},{9,13},{10,... | collective-permute-start | bytes 27656 | tf_op jit(solution)/shard_map/ppermute | solution.py:32
  67.7 7.2 %collective-permute-start.4 = (bf16[2,96,6,2,2]{1,4,3,2,0:T(2,128)(2,1)S(1)}, bf16[2,96,6,2,2]{1,4,3,2,0:T(2,128)(2,1)S(1)}, u32[]{:S(2)}, u32[]{:S(2)}) collective-permute-start(bf16[2,96,6,2,2]{1,4,3,2,0:T(2,128)(2,1)S(1)} %get-tuple-element.33), channel_id=1, source_target_pairs={{0,5},{1,4},{2,7},{3,6},{4,1},{5,0},{6,3},{7,2},{8,13},{9,12},{10,... | collective-permute-start | bytes 27656 | tf_op jit(solution)/shard_map/ppermute | solution.py:32
  69.4 6.1 %collective-permute-start.5 = (bf16[2,96,6,2,2]{1,4,3,2,0:T(2,128)(2,1)S(1)}, bf16[2,96,6,2,2]{1,4,3,2,0:T(2,128)(2,1)S(1)}, u32[]{:S(2)}, u32[]{:S(2)}) collective-permute-start(bf16[2,96,6,2,2]{1,4,3,2,0:T(2,128)(2,1)S(1)} %get-tuple-element.32), channel_id=1, source_target_pairs={{0,6},{1,7},{2,4},{3,5},{4,2},{5,3},{6,0},{7,1},{8,14},{9,15},{10,... | collective-permute-start | bytes 27656 | tf_op jit(solution)/shard_map/ppermute | solution.py:32
  69.9 8.9 %collective-permute-start.6 = (bf16[2,96,6,2,2]{1,4,3,2,0:T(2,128)(2,1)S(1)}, bf16[2,96,6,2,2]{1,4,3,2,0:T(2,128)(2,1)S(1)}, u32[]{:S(2)}, u32[]{:S(2)}) collective-permute-start(bf16[2,96,6,2,2]{1,4,3,2,0:T(2,128)(2,1)S(1)} %get-tuple-element.31), channel_id=1, source_target_pairs={{0,7},{1,6},{2,5},{3,4},{4,3},{5,2},{6,1},{7,0},{8,15},{9,14},{10,... | collective-permute-start | bytes 27656 | tf_op jit(solution)/shard_map/ppermute | solution.py:32
  72.2 7.5 %collective-permute-start.7 = (bf16[2,96,6,2,2]{1,4,3,2,0:T(2,128)(2,1)S(1)}, bf16[2,96,6,2,2]{1,4,3,2,0:T(2,128)(2,1)S(1)}, u32[]{:S(2)}, u32[]{:S(2)}) collective-permute-start(bf16[2,96,6,2,2]{1,4,3,2,0:T(2,128)(2,1)S(1)} %get-tuple-element.30), channel_id=1, source_target_pairs={{0,8},{1,9},{2,10},{3,11},{4,12},{5,13},{6,14},{7,15},{8,0},{9,1},... | collective-permute-start | bytes 27656 | tf_op jit(solution)/shard_map/ppermute | solution.py:32
  73.0 9.4 %collective-permute-start.8 = (bf16[2,96,6,2,2]{1,4,3,2,0:T(2,128)(2,1)S(1)}, bf16[2,96,6,2,2]{1,4,3,2,0:T(2,128)(2,1)S(1)}, u32[]{:S(2)}, u32[]{:S(2)}) collective-permute-start(bf16[2,96,6,2,2]{1,4,3,2,0:T(2,128)(2,1)S(1)} %get-tuple-element.29), channel_id=1, source_target_pairs={{0,9},{1,8},{2,11},{3,10},{4,13},{5,12},{6,15},{7,14},{8,1},{9,0},... | collective-permute-start | bytes 27656 | tf_op jit(solution)/shard_map/ppermute | solution.py:32
  75.0 8.9 %collective-permute-start.9 = (bf16[2,96,6,2,2]{1,4,3,2,0:T(2,128)(2,1)S(1)}, bf16[2,96,6,2,2]{1,4,3,2,0:T(2,128)(2,1)S(1)}, u32[]{:S(2)}, u32[]{:S(2)}) collective-permute-start(bf16[2,96,6,2,2]{1,4,3,2,0:T(2,128)(2,1)S(1)} %get-tuple-element.28), channel_id=1, source_target_pairs={{0,10},{1,11},{2,8},{3,9},{4,14},{5,15},{6,12},{7,13},{8,2},{9,3},... | collective-permute-start | bytes 27656 | tf_op jit(solution)/shard_map/ppermute | solution.py:32
  75.4 11.7 %collective-permute-start.10 = (bf16[2,96,6,2,2]{1,4,3,2,0:T(2,128)(2,1)S(1)}, bf16[2,96,6,2,2]{1,4,3,2,0:T(2,128)(2,1)S(1)}, u32[]{:S(2)}, u32[]{:S(2)}) collective-permute-start(bf16[2,96,6,2,2]{1,4,3,2,0:T(2,128)(2,1)S(1)} %get-tuple-element.27), channel_id=1, source_target_pairs={{0,11},{1,10},{2,9},{3,8},{4,15},{5,14},{6,13},{7,12},{8,3},{9,2},... | collective-permute-start | bytes 27656 | tf_op jit(solution)/shard_map/ppermute | solution.py:32
  78.8 8.4 %collective-permute-start.11 = (bf16[2,96,6,2,2]{1,4,3,2,0:T(2,128)(2,1)S(1)}, bf16[2,96,6,2,2]{1,4,3,2,0:T(2,128)(2,1)S(1)}, u32[]{:S(2)}, u32[]{:S(2)}) collective-permute-start(bf16[2,96,6,2,2]{1,4,3,2,0:T(2,128)(2,1)S(1)} %get-tuple-element.26), channel_id=1, source_target_pairs={{0,12},{1,13},{2,14},{3,15},{4,8},{5,9},{6,10},{7,11},{8,4},{9,5},... | collective-permute-start | bytes 27656 | tf_op jit(solution)/shard_map/ppermute | solution.py:32
  79.7 7.5 %collective-permute-start.12 = (bf16[2,96,6,2,2]{1,4,3,2,0:T(2,128)(2,1)S(1)}, bf16[2,96,6,2,2]{1,4,3,2,0:T(2,128)(2,1)S(1)}, u32[]{:S(2)}, u32[]{:S(2)}) collective-permute-start(bf16[2,96,6,2,2]{1,4,3,2,0:T(2,128)(2,1)S(1)} %get-tuple-element.25), channel_id=1, source_target_pairs={{0,13},{1,12},{2,15},{3,14},{4,9},{5,8},{6,11},{7,10},{8,5},{9,4},... | collective-permute-start | bytes 27656 | tf_op jit(solution)/shard_map/ppermute | solution.py:32
  82.4 6.5 %collective-permute-start.13 = (bf16[2,96,6,2,2]{1,4,3,2,0:T(2,128)(2,1)S(1)}, bf16[2,96,6,2,2]{1,4,3,2,0:T(2,128)(2,1)S(1)}, u32[]{:S(2)}, u32[]{:S(2)}) collective-permute-start(bf16[2,96,6,2,2]{1,4,3,2,0:T(2,128)(2,1)S(1)} %get-tuple-element.24), channel_id=1, source_target_pairs={{0,14},{1,15},{2,12},{3,13},{4,10},{5,11},{6,8},{7,9},{8,6},{9,7},... | collective-permute-start | bytes 27656 | tf_op jit(solution)/shard_map/ppermute | solution.py:32
  83.9 5.9 %collective-permute-start.14 = (bf16[2,96,6,2,2]{1,4,3,2,0:T(2,128)(2,1)S(1)}, bf16[2,96,6,2,2]{1,4,3,2,0:T(2,128)(2,1)S(1)}, u32[]{:S(2)}, u32[]{:S(2)}) collective-permute-start(bf16[2,96,6,2,2]{1,4,3,2,0:T(2,128)(2,1)S(1)} %get-tuple-element.23), channel_id=1, source_target_pairs={{0,15},{1,14},{2,13},{3,12},{4,11},{5,10},{6,9},{7,8},{8,7},{9,6},... | collective-permute-start | bytes 27656 | tf_op jit(solution)/shard_map/ppermute | solution.py:32
